TPU v7x, 512 devices: a whole 4x8x8 slice. The times are simulated.
512 devices in a mesh: gx: 8 (over y), gy: 8 (over x, core), gz: 8 (over z).
Axes of the slice: x: 4, y: 8, z: 8, core: 2. Of those that a mesh axis runs over, the one named last changes fastest.
Arguments:
- bricks: bfloat16 [4096, 2, 128, 128], P(('gx', 'gy', 'gz')), may hold values from -6 to 6
- live: int32 [4096], P(('gx', 'gy', 'gz')), may hold values from 1 to 2, as said below
- shear: float32 [4, 2], replicated, may hold values from -1 to 1
- offsets: int32 [4096, 4, 2], P(('gx', 'gy', 'gz')), may hold values from -8 to 8
- absorb: bfloat16 [4096], P(('gx', 'gy', 'gz')), may hold values from 0.019897461 to 0.119628906
- color_gain: float32 [3], replicated, may hold values from 0.5 to 3
- color_bias: float32 [3], replicated, may hold values from -1 to 1
- targets: int32 [4096, 4], P(('gx', 'gy', 'gz')), may hold values from 0 to 1023, as said below
- order: int32 [4, 4096], P(None, ('gx', 'gy', 'gz')), may hold values from 0 to 4095, each once within a row
Outputs:
- image: float32 [1024, 4, 128, 128], P(('gx', 'gy', 'gz'))
Inputs may be any that keep to these rules, and one draw needn't show every extreme that they name: Slices from live[b] on are empty; a device's rendering load can be up to twice another's. targets[b, v] = u has u mod 4 = v; tile u is owned by device u // 2 (devices counted in mesh order) and brick b by device b // 8, and both devices have the same gx index. A device sends at most 1 footprints to any one device; for each gx index some device receives 1 footprints from every device with that gx index. order[v] is a permutation of the bricks.
All inputs are finite; a program needn't handle non-finite values.
Results may differ from a plain program's by a relative error of at most 0.0016.
Values may be sent and summed in bfloat16 or wider, within the bound.
No kernel may reach another device: no remote copies, remote signals or barrier semaphores. Data moves between devices by JAX's collectives and lax.ppermute only.
A program may use at most 64 MiB of HBM per device.

v0:
```python
import jax
import jax.numpy as jnp
from jax import lax
from jax.experimental import pallas as pl
from jax.experimental.pallas import tpu as pltpu
from jax.sharding import PartitionSpec as P

SMEM = pltpu.SMEM
VMEM = pltpu.VMEM
F32 = jnp.float32
BF16 = jnp.bfloat16
META = 8
FIELDS = 8
PART = 32


def label_kernel(targets, order, offsets, live, absorb, bricks, block):
    views = targets.shape[0]
    rows = bricks.shape[1]
    slots = lax.axis_size("gy") * lax.axis_size("gz")
    lane = lax.broadcasted_iota(jnp.int32, (META, 128), 1)
    rates = absorb[...].astype(F32)
    spot = lax.broadcasted_iota(jnp.int32, rates.shape, 1)

    def one_brick(b, _):
        line = jnp.zeros((META, 128), F32)
        rate = jnp.sum(jnp.where(spot == b, rates, 0.0), axis=1, keepdims=True)
        for v in range(views):
            tile = targets[v, b]
            rank = order[v, b]
            fields = (
                (lax.rem(tile, 2) + 1).astype(F32),
                lax.div(rank, 64).astype(F32),
                lax.rem(rank, 64).astype(F32),
                offsets[v, 0, b].astype(F32),
                offsets[v, 1, b].astype(F32),
                live[b].astype(F32),
                rate,
                lax.rem(lax.div(tile, 2), slots).astype(F32),
            )
            for at, value in enumerate(fields):
                line = jnp.where(lane == v * FIELDS + at, value, line)
        block[b, 0:rows, :] = bricks[b]
        block[b, rows : rows + META, :] = line.astype(BF16)
        return 0

    lax.fori_loop(0, bricks.shape[0], one_brick, 0)


def pick_kernel(parts, *refs):
    blocks = refs[: len(parts)]
    send, names, names_s, sem = refs[len(parts) :]
    rows = send.shape[1] - META
    per = 1 + max(place for place, _ in parts)
    me = lax.axis_index("gz")
    planes = lax.axis_size("gz")
    start = 0
    for block in blocks:
        count = block.shape[0]
        lines = jnp.max(block[:, rows : rows + META, :].astype(F32), axis=1)
        names[start : start + count, :] = lines.astype(jnp.int32)
        start += count
    copy = pltpu.make_async_copy(names, names_s, sem)
    copy.start()
    for slot in range(send.shape[0]):
        send[slot, rows : rows + META, :] = jnp.zeros((META, 128), BF16)
    copy.wait()
    start = 0
    for block, (place, _) in zip(blocks, parts):

        def one_brick(b, _, block=block, place=place, start=start):
            for v in range(4):
                goal = names_s[start + b, v * FIELDS + FIELDS - 1]

                @pl.when(lax.rem(goal, planes) == me)
                def _():
                    slot = lax.div(goal, planes) * per + place
                    send[slot, 0:rows, :] = block[b, 0:rows, :]
                    line = block[b, rows : rows + META, :].astype(F32)
                    if v:
                        line = pltpu.roll(line, 128 - v * FIELDS, 1)
                    send[slot, rows : rows + META, :] = line.astype(BF16)

            return 0

        lax.fori_loop(0, block.shape[0], one_brick, 0)
        start += block.shape[0]


def as_row(column, count, empty=0.0):
    lane = lax.broadcasted_iota(jnp.int32, (count, 128), 1)
    line = lax.broadcasted_iota(jnp.int32, (count, 128), 0)
    wide = jnp.broadcast_to(column, (count, 128))
    row = jnp.sum(jnp.where(lane == line, wide, 0.0), axis=0, keepdims=True)
    if empty:
        row = jnp.where(lane[0:1] < count, row, empty)
    return row


def order_of(key, count):
    lane = lax.broadcasted_iota(jnp.int32, (count, 128), 1)
    line = lax.broadcasted_iota(jnp.int32, (count, 128), 0).astype(F32)
    row = as_row(key, count, 1e9)
    place = jnp.sum(jnp.where(row < key, 1.0, 0.0), axis=1, keepdims=True)
    hit = place.astype(jnp.int32) == lane
    return jnp.sum(jnp.where(hit, line, 0.0), axis=0, keepdims=True)


def plan(meta, first, ints, reals):
    count = meta.shape[0]
    lane = lax.broadcasted_iota(jnp.int32, (count, 128), 1)
    index = lax.broadcasted_iota(jnp.int32, (count, 1), 0).astype(F32)

    def field(at):
        return jnp.sum(jnp.where(lane == at, meta, 0.0), axis=1, keepdims=True)

    def total(mask):
        zero = jnp.zeros((1, 128), F32)
        return zero + jnp.sum(jnp.where(mask, 1.0, 0.0), axis=0, keepdims=True)

    tile_1 = field(0)
    rank = field(1) * 64.0 + field(2)
    live = field(5)
    valid = tile_1 > 0.5
    fresh = valid & (index > first - 0.5)
    by_live = jnp.where(fresh, live * 256.0 + index, 4096.0 + index)
    by_rank = jnp.where(valid, tile_1 * 4096.0 + rank, 16384.0 + index)
    rows = (
        order_of(by_live, count),
        order_of(by_rank, count),
        total(fresh & (live < 1.5)),
        total(fresh),
        total(valid),
        total(valid & (tile_1 < 1.5)),
        as_row(tile_1, count),
    )
    for at, row in enumerate(rows):
        ints[at : at + 1, :] = row.astype(jnp.int32)
    for at, row in enumerate((field(3), field(4), field(6))):
        reals[at : at + 1, :] = as_row(row, count)


def draw_all(shear, gain, bias, recv, first, feet, bufs, ints_s, reals_s):
    extent = recv.shape[2]
    layers = (recv.shape[1] - META) // extent
    view_base = 2 * lax.rem(lax.axis_index("gz"), 2)
    apart = (
        lax.broadcasted_iota(jnp.int32, (extent, extent), 0)
        - lax.broadcasted_iota(jnp.int32, (extent, extent), 1)
    ).astype(F32)
    gains = [0.5 * gain[c] for c in range(3)]
    biases = [0.5 * bias[c] for c in range(3)]

    def density(slot, layer, out):
        view = view_base + ints_s[6, slot] - 1
        raised = F32(layer - layers // 2)
        sx = reals_s[0, slot] + raised * shear[0, view]
        sy = reals_s[1, slot] + raised * shear[1, view]
        across = jnp.maximum(0.0, 1.0 - jnp.abs(apart - sx)).astype(BF16)
        downward = jnp.maximum(0.0, 1.0 - jnp.abs(apart + sy)).astype(BF16)
        source = recv[slot - first, layer * extent : (layer + 1) * extent, :]
        halfway = jnp.dot(across, source, preferred_element_type=F32).astype(BF16)
        out[...] = jnp.dot(halfway, downward, preferred_element_type=F32)

    def shade(slot, dens):
        rate = reals_s[2, slot]
        for begin in range(0, extent, PART):
            span = slice(begin, begin + PART)
            colors = [None] * 3
            through = None
            for one in dens:
                d = one[span, :]
                thick = rate * jnp.log(1.0 + jnp.exp(d))
                pass_on = jnp.exp(-thick)
                half = 0.5 - 0.5 * pass_on
                if through is None:
                    through = pass_on
                    optical = thick
                else:
                    half = through * half
                    optical = optical + thick
                for c in range(3):
                    now = half * jnp.tanh(gains[c] * d + biases[c]) + half
                    colors[c] = now if colors[c] is None else colors[c] + now
            for c in range(3):
                feet[slot, c, span, :] = colors[c].astype(BF16)
            feet[slot, 3, span, :] = optical.astype(BF16)

    def render(begin, end, layer_count, bufs_a, bufs_b):
        def fill(at, dens):
            slot = ints_s[0, jnp.minimum(at, end - 1)]
            for layer in range(layer_count):
                density(slot, layer, dens[layer])

        def draw(at, dens):
            shade(ints_s[0, jnp.minimum(at, end - 1)], dens[:layer_count])

        @pl.when(end > begin)
        def _():
            fill(begin, bufs_a)

            def two(step, _):
                at = begin + 2 * step
                fill(at + 1, bufs_b)
                draw(at, bufs_a)
                fill(at + 2, bufs_a)
                draw(at + 1, bufs_b)
                return 0

            lax.fori_loop(0, lax.div(end - begin + 1, 2), two, 0)

    short_n = ints_s[2, 0]
    fresh_n = ints_s[3, 0]
    render(0, short_n, 1, bufs[0:1], bufs[2:3])
    render(short_n, fresh_n, 2, bufs[0:2], bufs[2:4])


def render_kernel(shear, gain, bias, recv, feet, b0, b1, b2, b3, ints, reals, ints_s, reals_s, sems):
    rows = recv.shape[1] - META
    meta = jnp.max(recv[:, rows : rows + META, :].astype(F32), axis=1)
    plan(meta, 0, ints, reals)
    copies = [
        pltpu.make_async_copy(ints, ints_s, sems.at[0]),
        pltpu.make_async_copy(reals, reals_s, sems.at[1]),
    ]
    for copy in copies:
        copy.start()
    for copy in copies:
        copy.wait()
    draw_all(shear, gain, bias, recv, 0, feet, (b0, b1, b2, b3), ints_s, reals_s)


def paint_kernel(*refs):
    shear, gain, bias = refs[:3]
    (image, feet, b0, b1, b2, b3, lines, ints, reals, ints_s, reals_s, sems) = refs[-12:]
    middle = refs[3:-12]
    recv = middle[-1]
    done = len(middle) // 2
    extent = recv.shape[2]
    rows = recv.shape[1] - META
    first = 0
    meta_copies, feet_copies = [], []
    for group in range(done):
        old, old_feet = middle[2 * group], middle[2 * group + 1]
        count = old.shape[0]
        span = pl.ds(first, count)
        meta_copies.append(
            pltpu.make_async_copy(
                old.at[:, pl.ds(rows, META), :], lines.at[span], sems.at[2 * group + 2]
            )
        )
        feet_copies.append(
            pltpu.make_async_copy(old_feet, feet.at[span], sems.at[2 * group + 3])
        )
        first += count
    for copy in meta_copies + feet_copies:
        copy.start()
    lines[first : first + recv.shape[0]] = recv[:, rows : rows + META, :]
    image[...] = jnp.zeros_like(image)
    for copy in meta_copies:
        copy.wait()
    meta = jnp.max(lines[...].astype(F32), axis=1)
    plan(meta, first, ints, reals)
    copies = [
        pltpu.make_async_copy(ints, ints_s, sems.at[0]),
        pltpu.make_async_copy(reals, reals_s, sems.at[1]),
    ]
    for copy in copies:
        copy.start()
    for copy in copies:
        copy.wait()
    draw_all(shear, gain, bias, recv, first, feet, (b0, b1, b2, b3), ints_s, reals_s)
    for copy in feet_copies:
        copy.wait()

    all_n = ints_s[4, 0]
    first_n = ints_s[5, 0]
    for tile in range(2):

        def lay(at, _):
            slot = ints_s[1, at]
            for begin in range(0, extent, PART):
                span = slice(begin, begin + PART)
                optical = image[tile, 3, span, :]
                through = jnp.exp(-optical)
                for c in range(3):
                    image[tile, c, span, :] += through * feet[slot, c, span, :].astype(F32)
                image[tile, 3, span, :] = optical + feet[slot, 3, span, :].astype(F32)
            return 0

        begin, end = (0, first_n) if tile == 0 else (first_n, all_n)
        lax.fori_loop(begin, end, lay, 0)
        image[tile, 3, :, :] = jnp.exp(-image[tile, 3, :, :])


def body(bricks, live, shear, offsets, absorb, color_gain, color_bias, targets, order):
    count, layers, extent, _ = bricks.shape
    rows = layers * extent
    columns = lax.axis_size("gy")
    planes = lax.axis_size("gz")
    smem = pl.BlockSpec(memory_space=SMEM)
    vmem = pl.BlockSpec(memory_space=VMEM)
    here = pl.BlockSpec(memory_space=pl.ANY)
    square = VMEM((extent, extent), F32)
    tables = [
        square,
        square,
        square,
        square,
    ]
    small = [
        VMEM((8, 128), jnp.int32),
        VMEM((8, 128), F32),
        SMEM((8, 128), jnp.int32),
        SMEM((8, 128), F32),
    ]
    block = pl.pallas_call(
        label_kernel,
        name="label",
        out_shape=jax.ShapeDtypeStruct((count, rows + META, extent), BF16),
        in_specs=[smem] * 4 + [vmem] * 2,
        out_specs=vmem,
    )(
        targets.T,
        order,
        offsets.transpose(1, 2, 0),
        live,
        absorb.reshape(1, count),
        bricks.reshape(count, rows, extent),
    )

    def move(what, step):
        return lax.ppermute(what, "gz", [(z, (z + step) % planes) for z in range(planes)])

    def pick(parts, blocks):
        per = 1 + max(place for place, _ in parts)
        total = sum(b.shape[0] for b in blocks)
        return pl.pallas_call(
            lambda *refs: pick_kernel(parts, *refs),
            name="pick",
            out_shape=jax.ShapeDtypeStruct((columns * per, rows + META, extent), BF16),
            in_specs=[vmem] * len(blocks),
            out_specs=vmem,
            scratch_shapes=[
                VMEM((total, 128), jnp.int32),
                SMEM((total, 128), jnp.int32),
                pltpu.SemaphoreType.DMA,
            ],
            cost_estimate=pl.CostEstimate(flops=0, bytes_accessed=6_000_000, transcendentals=0),
        )(*blocks)

    def spread(what):
        return lax.all_to_all(what, "gy", split_axis=0, concat_axis=0, tiled=True)

    def render(recv):
        slots = recv.shape[0]
        return pl.pallas_call(
            render_kernel,
            name="render",
            out_shape=jax.ShapeDtypeStruct((slots, 4, extent, extent), BF16),
            in_specs=[smem] * 3 + [vmem],
            out_specs=vmem,
            scratch_shapes=tables + small + [pltpu.SemaphoreType.DMA((2,))],
            cost_estimate=pl.CostEstimate(flops=0, bytes_accessed=8_000_000, transcendentals=0),
        )(shear.T, color_gain, color_bias, recv)

    half = count // 2
    ups, downs = [block], [block]
    for _ in range(1, planes // 2):
        ups.append(move(ups[-1], 1))
        downs.append(move(downs[-1], -1))
    up_far = move(ups[-1][:half], 1)
    down_far = move(downs[-1][half:], -1)

    groups = (
        (((0, 0),), (block,)),
        (((0, 0), (1, 0)), (ups[1], downs[1])),
        (((0, 0), (1, 0)), (ups[2], downs[2])),
        (((0, 0), (1, 0), (2, 0), (2, 0)), (ups[3], downs[3], up_far, down_far)),
    )
    received = []
    for parts, blocks in groups:
        send = pick(parts, blocks)
        received.append(spread(send))
    slots = sum(r.shape[0] for r in received)
    middle = []
    for recv in received[:-1]:
        middle += [recv, render(recv)]
    return pl.pallas_call(
        paint_kernel,
        name="paint",
        out_shape=jax.ShapeDtypeStruct((2, 4, extent, extent), F32),
        in_specs=[smem] * 3 + [here] * len(middle) + [vmem],
        out_specs=vmem,
        scratch_shapes=[VMEM((slots, 4, extent, extent), BF16)]
        + tables
        + [VMEM((slots, META, 128), BF16)]
        + small
        + [pltpu.SemaphoreType.DMA((2 + len(middle),))],
    )(shear.T, color_gain, color_bias, *middle, received[-1])


def solution(mesh):
    whole = ("gx", "gy", "gz")
    placed = (
        P(whole, None, None, None),
        P(whole),
        P(),
        P(whole, None, None),
        P(whole),
        P(),
        P(),
        P(whole, None),
        P(None, whole),
    )

    return jax.shard_map(
        body,
        mesh=mesh,
        in_specs=placed,
        out_specs=P(whole, None, None, None),
        check_vma=False,
    )
```

profile of v0, /device:TPU:38, one launch (start us, length us, event | category | flops | bytes accessed | tf_op | source)
XLA Modules:
  0.0 144.8 jit_solution(9274922976902810212)
XLA Ops:
  0.0 2.6 %label.1.refs_0_ = bf16[8,264,128]{2,1,0:T(8,128)(2,1)} custom-call(s32[4,8]{1,0:T(4,128)} %bitcast.11, s32[4,8]{1,0:T(4,128)} %order.1, s32[4,2,8]{2,1,0:T(2,128)} %bitcast.10, s32[8]{0:T(128)} %live.1, bf16[1,8]{1,0:T(2,128)(2,1)} %bitcast.12, bf16[8,256,128]{2,1,0:T(8,128)(2,1)} %bitcast.5), custom_call_target="tpu_custom_call" | custom-call | tf_op jit(solution)/shard_map/label/pallas_call | solution.py:317
  2.6 10.9 %collective-permute-start.1 = (bf16[8,264,128]{2,1,0:T(8,128)(2,1)}, bf16[8,264,128]{2,1,0:T(8,128)(2,1)S(1)}, u32[]{:S(2)}, u32[]{:S(2)}) collective-permute-start(bf16[8,264,128]{2,1,0:T(8,128)(2,1)} %label.1.refs_0_), channel_id=1, source_target_pairs={{0,7},{1,0},{2,1},{3,2},{4,3},{5,4},{6,5},{7,6},{8,15},{9,8},{10,9... | collective-permute-start | bytes 1622024 | tf_op jit(solution)/shard_map/ppermute | solution.py:333
  13.6 1.9 %collective-permute-start = (bf16[8,264,128]{2,1,0:T(8,128)(2,1)}, bf16[8,264,128]{2,1,0:T(8,128)(2,1)S(1)}, u32[]{:S(2)}, u32[]{:S(2)}) collective-permute-start(bf16[8,264,128]{2,1,0:T(8,128)(2,1)} %label.1.refs_0_), channel_id=1, source_target_pairs={{0,1},{1,2},{2,3},{3,4},{4,5},{5,6},{6,7},{7,0},{8,9},{9,10},{10,1... | collective-permute-start | bytes 1622024 | tf_op jit(solution)/shard_map/ppermute | solution.py:333
  15.5 2.9 %pick.4 = bf16[8,264,128]{2,1,0:T(8,128)(2,1)} custom-call(bf16[8,264,128]{2,1,0:T(8,128)(2,1)} %label.1.refs_0_), custom_call_target="tpu_custom_call" | custom-call | bytes 6000000 | tf_op jit(solution)/shard_map/pick/pallas_call | solution.py:338
  18.5 4.8 %all-to-all-start = ((bf16[8,264,128]{2,1,0:T(8,128)(2,1)}), bf16[8,264,128]{2,1,0:T(8,128)(2,1)S(1)}, u32[]{:S(2)}, u32[]{:S(2)}) async-start(bf16[8,264,128]{2,1,0:T(8,128)(2,1)} %pick.4), calls=%async_computation | async-start | bytes 1081344 | tf_op jit(solution)/shard_map/all_to_all | solution.py:353
  23.2 2.2 %collective-permute-done.1.refs_1_ = bf16[8,264,128]{2,1,0:T(8,128)(2,1)S(1)} collective-permute-done((bf16[8,264,128]{2,1,0:T(8,128)(2,1)}, bf16[8,264,128]{2,1,0:T(8,128)(2,1)S(1)}, u32[]{:S(2)}, u32[]{:S(2)}) %collective-permute-start.1) | collective-permute-done | bytes 540704 | tf_op jit(solution)/shard_map/ppermute | solution.py:333
  25.4 0.0 copy-start.5
  25.4 5.2 %collective-permute-done.refs_0_ = bf16[8,264,128]{2,1,0:T(8,128)(2,1)S(1)} collective-permute-done((bf16[8,264,128]{2,1,0:T(8,128)(2,1)}, bf16[8,264,128]{2,1,0:T(8,128)(2,1)S(1)}, u32[]{:S(2)}, u32[]{:S(2)}) %collective-permute-start) | collective-permute-done | bytes 540704 | tf_op jit(solution)/shard_map/ppermute | solution.py:333
  30.6 0.0 copy-done.5
  30.6 0.0 copy-start.7
  30.6 0.8 copy-done.7
  31.4 3.9 %pick.5 = bf16[16,264,128]{2,1,0:T(8,128)(2,1)} custom-call(bf16[8,264,128]{2,1,0:T(8,128)(2,1)} %copy-done.7, bf16[8,264,128]{2,1,0:T(8,128)(2,1)} %copy-done.5), custom_call_target="tpu_custom_call" | custom-call | bytes 6000000 | tf_op jit(solution)/shard_map/pick/pallas_call | solution.py:338
  35.3 0.0 copy-start.6
  35.3 0.0 copy-start.8
  35.3 0.0 all-to-all-done.recv.refs_3_
  35.4 0.0 copy-start.2
  35.4 4.9 %all-to-all-start.1 = ((bf16[16,264,128]{2,1,0:T(8,128)(2,1)}), bf16[16,264,128]{2,1,0:T(8,128)(2,1)S(1)}, u32[]{:S(2)}, u32[]{:S(2)}) async-start(bf16[16,264,128]{2,1,0:T(8,128)(2,1)} %pick.5), calls=%async_computation.1 | async-start | bytes 2162688 | tf_op jit(solution)/shard_map/all_to_all | solution.py:353
  40.2 0.0 copy-done.6
  40.2 2.1 %collective-permute-start.3 = (bf16[8,264,128]{2,1,0:T(8,128)(2,1)S(1)}, bf16[8,264,128]{2,1,0:T(8,128)(2,1)}, u32[]{:S(2)}, u32[]{:S(2)}) collective-permute-start(bf16[8,264,128]{2,1,0:T(8,128)(2,1)S(1)} %copy-done.6), channel_id=1, source_target_pairs={{0,7},{1,0},{2,1},{3,2},{4,3},{5,4},{6,5},{7,6},{8,15},{9,8},{10,9... | collective-permute-start | bytes 1622024 | tf_op jit(solution)/shard_map/ppermute | solution.py:333
  42.4 0.0 copy-done.8
  42.4 3.7 %collective-permute-start.2 = (bf16[8,264,128]{2,1,0:T(8,128)(2,1)S(1)}, bf16[8,264,128]{2,1,0:T(8,128)(2,1)S(1)}, u32[]{:S(2)}, u32[]{:S(2)}) collective-permute-start(bf16[8,264,128]{2,1,0:T(8,128)(2,1)S(1)} %copy-done.8), channel_id=1, source_target_pairs={{0,1},{1,2},{2,3},{3,4},{4,5},{5,6},{6,7},{7,0},{8,9},{9,10},{10,1... | collective-permute-start | bytes 1622024 | tf_op jit(solution)/shard_map/ppermute | solution.py:333
  46.1 10.4 %collective-permute-done.3.refs_1_ = bf16[8,264,128]{2,1,0:T(8,128)(2,1)} collective-permute-done((bf16[8,264,128]{2,1,0:T(8,128)(2,1)S(1)}, bf16[8,264,128]{2,1,0:T(8,128)(2,1)}, u32[]{:S(2)}, u32[]{:S(2)}) %collective-permute-start.3) | collective-permute-done | bytes 540704 | tf_op jit(solution)/shard_map/ppermute | solution.py:333
  56.5 3.0 %collective-permute-done.2.refs_0_ = bf16[8,264,128]{2,1,0:T(8,128)(2,1)S(1)} collective-permute-done((bf16[8,264,128]{2,1,0:T(8,128)(2,1)S(1)}, bf16[8,264,128]{2,1,0:T(8,128)(2,1)S(1)}, u32[]{:S(2)}, u32[]{:S(2)}) %collective-permute-start.2) | collective-permute-done | bytes 540704 | tf_op jit(solution)/shard_map/ppermute | solution.py:333
  59.6 0.0 copy-start.9
  59.6 0.8 copy-done.9
  60.4 3.9 %pick.6 = bf16[16,264,128]{2,1,0:T(8,128)(2,1)} custom-call(bf16[8,264,128]{2,1,0:T(8,128)(2,1)} %copy-done.9, bf16[8,264,128]{2,1,0:T(8,128)(2,1)} %collective-permute-done.3.refs_1_), custom_call_target="tpu_custom_call" | custom-call | bytes 6000000 | tf_op jit(solution)/shard_map/pick/pallas_call | solution.py:338
  64.2 0.0 copy-done.2
  64.2 0.0 all-to-all-done.1.recv.refs_5_
  64.3 0.0 copy-start
  64.3 4.8 %all-to-all-start.2 = ((bf16[16,264,128]{2,1,0:T(8,128)(2,1)}), bf16[16,264,128]{2,1,0:T(8,128)(2,1)S(1)}, u32[]{:S(2)}, u32[]{:S(2)}) async-start(bf16[16,264,128]{2,1,0:T(8,128)(2,1)} %pick.6), calls=%async_computation.2 | async-start | bytes 2162688 | tf_op jit(solution)/shard_map/all_to_all | solution.py:353
  69.1 1.9 %collective-permute-start.5 = (bf16[8,264,128]{2,1,0:T(8,128)(2,1)}, bf16[8,264,128]{2,1,0:T(8,128)(2,1)S(1)}, u32[]{:S(2)}, u32[]{:S(2)}) collective-permute-start(bf16[8,264,128]{2,1,0:T(8,128)(2,1)} %collective-permute-done.3.refs_1_), channel_id=1, source_target_pairs={{0,7},{1,0},{2,1},{3,2},{4,3},{5,4},{6,5},{7,6},{8,15},{9,8},{10,9... | collective-permute-start | bytes 1622024 | tf_op jit(solution)/shard_map/ppermute | solution.py:333
  71.0 3.9 %collective-permute-start.4 = (bf16[8,264,128]{2,1,0:T(8,128)(2,1)}, bf16[8,264,128]{2,1,0:T(8,128)(2,1)S(1)}, u32[]{:S(2)}, u32[]{:S(2)}) collective-permute-start(bf16[8,264,128]{2,1,0:T(8,128)(2,1)} %copy-done.9), channel_id=1, source_target_pairs={{0,1},{1,2},{2,3},{3,4},{4,5},{5,6},{6,7},{7,0},{8,9},{9,10},{10,1... | collective-permute-start | bytes 1622024 | tf_op jit(solution)/shard_map/ppermute | solution.py:333
  74.9 10.5 %collective-permute-done.5.refs_1_ = bf16[8,264,128]{2,1,0:T(8,128)(2,1)S(1)} collective-permute-done((bf16[8,264,128]{2,1,0:T(8,128)(2,1)}, bf16[8,264,128]{2,1,0:T(8,128)(2,1)S(1)}, u32[]{:S(2)}, u32[]{:S(2)}) %collective-permute-start.5) | collective-permute-done | bytes 540704 | tf_op jit(solution)/shard_map/ppermute | solution.py:333
  85.5 0.0 copy-start.3
  85.5 3.4 %collective-permute-start.7 = (bf16[4,264,128]{2,1,0:T(8,128)(2,1)S(1)}, bf16[4,264,128]{2,1,0:T(8,128)(2,1)S(1)}, u32[]{:S(2)}, u32[]{:S(2)}) collective-permute-start(bf16[4,264,128]{2,1,0:T(8,128)(2,1)S(1)} %slice.9), channel_id=1, source_target_pairs={{0,7},{1,0},{2,1},{3,2},{4,3},{5,4},{6,5},{7,6},{8,15},{9,8},{10,9... | collective-permute-start | bytes 811016 | tf_op jit(solution)/shard_map/ppermute | solution.py:333
  88.9 0.0 collective-permute-done.4.refs_0_
  88.9 0.0 copy-start.4
  89.0 0.0 copy-done
  89.0 2.4 %collective-permute-start.6 = (bf16[4,264,128]{2,1,0:T(8,128)(2,1)S(1)}, bf16[4,264,128]{2,1,0:T(8,128)(2,1)}, u32[]{:S(2)}, u32[]{:S(2)}) collective-permute-start(bf16[4,264,128]{2,1,0:T(8,128)(2,1)S(1)} %slice.8), channel_id=1, source_target_pairs={{0,1},{1,2},{2,3},{3,4},{4,5},{5,6},{6,7},{7,0},{8,9},{9,10},{10,1... | collective-permute-start | bytes 811016 | tf_op jit(solution)/shard_map/ppermute | solution.py:333
  91.4 3.6 %collective-permute-done.7.refs_3_ = bf16[4,264,128]{2,1,0:T(8,128)(2,1)S(1)} collective-permute-done((bf16[4,264,128]{2,1,0:T(8,128)(2,1)S(1)}, bf16[4,264,128]{2,1,0:T(8,128)(2,1)S(1)}, u32[]{:S(2)}, u32[]{:S(2)}) %collective-permute-start.7) | collective-permute-done | bytes 270368 | tf_op jit(solution)/shard_map/ppermute | solution.py:333
  95.0 0.0 copy-start.10
  95.0 4.8 %collective-permute-done.6.refs_2_ = bf16[4,264,128]{2,1,0:T(8,128)(2,1)} collective-permute-done((bf16[4,264,128]{2,1,0:T(8,128)(2,1)S(1)}, bf16[4,264,128]{2,1,0:T(8,128)(2,1)}, u32[]{:S(2)}, u32[]{:S(2)}) %collective-permute-start.6) | collective-permute-done | bytes 270368 | tf_op jit(solution)/shard_map/ppermute | solution.py:333
  99.8 0.0 copy-done.3
  99.8 0.0 copy-done.4
  99.8 0.0 copy-done.10
  99.9 4.7 %pick.7 = bf16[24,264,128]{2,1,0:T(8,128)(2,1)} custom-call(bf16[8,264,128]{2,1,0:T(8,128)(2,1)} %copy-done.4, bf16[8,264,128]{2,1,0:T(8,128)(2,1)} %copy-done.3, bf16[4,264,128]{2,1,0:T(8,128)(2,1)} %collective-permute-done.6.refs_2_, bf16[4,264,128]{2,1,0:T(8,128)(2,1)} %copy-done.10), custom_call_target="tpu_custom_call" | custom-call | bytes 6000000 | tf_op jit(solution)/shard_map/pick/pallas_call | solution.py:338
  104.6 0.0 all-to-all-done.2.recv.refs_7_
  104.6 0.0 copy-start.1
  104.6 1.0 copy-done.1
  105.6 5.0 %all-to-all-start.3 = ((bf16[24,264,128]{2,1,0:T(8,128)(2,1)}), bf16[24,264,128]{2,1,0:T(8,128)(2,1)}, u32[]{:S(2)}, u32[]{:S(2)}) async-start(bf16[24,264,128]{2,1,0:T(8,128)(2,1)} %pick.7), calls=%async_computation.3 | async-start | bytes 3244032 | tf_op jit(solution)/shard_map/all_to_all | solution.py:353
  110.7 5.7 %render.3.refs_4_ = bf16[8,4,128,128]{3,2,1,0:T(8,128)(2,1)} custom-call(f32[2,4]{1,0:T(2,128)} %bitcast.6, f32[3]{0:T(128)} %refs_1_.1, f32[3]{0:T(128)} %refs_2_.1, bf16[8,264,128]{2,1,0:T(8,128)(2,1)} %copy-done.2), custom_call_target="tpu_custom_call" | custom-call | bytes 8000000 | tf_op jit(solution)/shard_map/render/pallas_call | solution.py:357
  116.4 7.9 %render.4.refs_6_ = bf16[16,4,128,128]{3,2,1,0:T(8,128)(2,1)} custom-call(f32[2,4]{1,0:T(2,128)} %bitcast.7, f32[3]{0:T(128)} %refs_1_.1, f32[3]{0:T(128)} %refs_2_.1, bf16[16,264,128]{2,1,0:T(8,128)(2,1)} %copy-done), custom_call_target="tpu_custom_call" | custom-call | bytes 8000000 | tf_op jit(solution)/shard_map/render/pallas_call | solution.py:357
  124.3 7.7 %render.5.refs_8_ = bf16[16,4,128,128]{3,2,1,0:T(8,128)(2,1)} custom-call(f32[2,4]{1,0:T(2,128)} %bitcast.8, f32[3]{0:T(128)} %refs_1_.1, f32[3]{0:T(128)} %refs_2_.1, bf16[16,264,128]{2,1,0:T(8,128)(2,1)} %copy-done.1), custom_call_target="tpu_custom_call" | custom-call | bytes 8000000 | tf_op jit(solution)/shard_map/render/pallas_call | solution.py:357
  132.1 0.0 all-to-all-done.3.refs_9_
  132.1 12.7 %paint.1 = f32[2,4,128,128]{3,2,1,0:T(8,128)} custom-call(f32[2,4]{1,0:T(2,128)} %bitcast.9, f32[3]{0:T(128)} %refs_1_.1, f32[3]{0:T(128)} %refs_2_.1, bf16[8,264,128]{2,1,0:T(8,128)(2,1)} %copy-done.2, bf16[8,4,128,128]{3,2,1,0:T(8,128)(2,1)} %render.3.refs_4_, bf16[16,264,128]{2,1,0:T(8,128)(2,1)} %copy-done, bf16[16,4,128,128]{3,2,1,0:T(8,128)(2,1)} %render.4.refs_6_, ...), custom_call_target="tpu_custom_call" | custom-call | tf_op jit(solution)/shard_map/paint/pallas_call | solution.py:389
  (2 shorter events, 0.0 us)
Async XLA Ops:
  2.6 22.8 %collective-permute-start.1 = (bf16[8,264,128]{2,1,0:T(8,128)(2,1)}, bf16[8,264,128]{2,1,0:T(8,128)(2,1)S(1)}, u32[]{:S(2)}, u32[]{:S(2)}) collective-permute-start(bf16[8,264,128]{2,1,0:T(8,128)(2,1)} %label.1.refs_0_), channel_id=1, source_target_pairs={{0,7},{1,0},{2,1},{3,2},{4,3},{5,4},{6,5},{7,6},{8,15},{9,8},{10,9... | collective-permute-start | bytes 1622024 | tf_op jit(solution)/shard_map/ppermute | solution.py:333
  13.6 17.0 %collective-permute-start = (bf16[8,264,128]{2,1,0:T(8,128)(2,1)}, bf16[8,264,128]{2,1,0:T(8,128)(2,1)S(1)}, u32[]{:S(2)}, u32[]{:S(2)}) collective-permute-start(bf16[8,264,128]{2,1,0:T(8,128)(2,1)} %label.1.refs_0_), channel_id=1, source_target_pairs={{0,1},{1,2},{2,3},{3,4},{4,5},{5,6},{6,7},{7,0},{8,9},{9,10},{10,1... | collective-permute-start | bytes 1622024 | tf_op jit(solution)/shard_map/ppermute | solution.py:333
  18.5 16.9 %all-to-all-start = ((bf16[8,264,128]{2,1,0:T(8,128)(2,1)}), bf16[8,264,128]{2,1,0:T(8,128)(2,1)S(1)}, u32[]{:S(2)}, u32[]{:S(2)}) async-start(bf16[8,264,128]{2,1,0:T(8,128)(2,1)} %pick.4), calls=%async_computation | async-start | bytes 1081344 | tf_op jit(solution)/shard_map/all_to_all | solution.py:353
  25.4 5.2 %copy-start.5 = (bf16[8,264,128]{2,1,0:T(8,128)(2,1)}, bf16[8,264,128]{2,1,0:T(8,128)(2,1)S(1)}, u32[]{:S(2)}) copy-start(bf16[8,264,128]{2,1,0:T(8,128)(2,1)S(1)} %collective-permute-done.1.refs_1_) | copy-start | bytes 1622020
  30.6 0.8 copy-start.7
  35.3 4.9 %copy-start.6 = (bf16[8,264,128]{2,1,0:T(8,128)(2,1)S(1)}, bf16[8,264,128]{2,1,0:T(8,128)(2,1)}, u32[]{:S(2)}) copy-start(bf16[8,264,128]{2,1,0:T(8,128)(2,1)} %copy-done.5) | copy-start | bytes 1622020
  35.3 7.1 %copy-start.8 = (bf16[8,264,128]{2,1,0:T(8,128)(2,1)S(1)}, bf16[8,264,128]{2,1,0:T(8,128)(2,1)}, u32[]{:S(2)}) copy-start(bf16[8,264,128]{2,1,0:T(8,128)(2,1)} %copy-done.7) | copy-start | bytes 1622020
  35.4 28.9 %copy-start.2 = (bf16[8,264,128]{2,1,0:T(8,128)(2,1)}, bf16[8,264,128]{2,1,0:T(8,128)(2,1)S(1)}, u32[]{:S(2)}) copy-start(bf16[8,264,128]{2,1,0:T(8,128)(2,1)S(1)} %all-to-all-done.recv.refs_3_) | copy-start | bytes 1622020
  35.4 28.9 %all-to-all-start.1 = ((bf16[16,264,128]{2,1,0:T(8,128)(2,1)}), bf16[16,264,128]{2,1,0:T(8,128)(2,1)S(1)}, u32[]{:S(2)}, u32[]{:S(2)}) async-start(bf16[16,264,128]{2,1,0:T(8,128)(2,1)} %pick.5), calls=%async_computation.1 | async-start | bytes 2162688 | tf_op jit(solution)/shard_map/all_to_all | solution.py:353
  40.2 16.3 %collective-permute-start.3 = (bf16[8,264,128]{2,1,0:T(8,128)(2,1)S(1)}, bf16[8,264,128]{2,1,0:T(8,128)(2,1)}, u32[]{:S(2)}, u32[]{:S(2)}) collective-permute-start(bf16[8,264,128]{2,1,0:T(8,128)(2,1)S(1)} %copy-done.6), channel_id=1, source_target_pairs={{0,7},{1,0},{2,1},{3,2},{4,3},{5,4},{6,5},{7,6},{8,15},{9,8},{10,9... | collective-permute-start | bytes 1622024 | tf_op jit(solution)/shard_map/ppermute | solution.py:333
  42.4 17.2 %collective-permute-start.2 = (bf16[8,264,128]{2,1,0:T(8,128)(2,1)S(1)}, bf16[8,264,128]{2,1,0:T(8,128)(2,1)S(1)}, u32[]{:S(2)}, u32[]{:S(2)}) collective-permute-start(bf16[8,264,128]{2,1,0:T(8,128)(2,1)S(1)} %copy-done.8), channel_id=1, source_target_pairs={{0,1},{1,2},{2,3},{3,4},{4,5},{5,6},{6,7},{7,0},{8,9},{9,10},{10,1... | collective-permute-start | bytes 1622024 | tf_op jit(solution)/shard_map/ppermute | solution.py:333
  59.6 0.8 copy-start.9
  64.3 24.7 %copy-start = (bf16[16,264,128]{2,1,0:T(8,128)(2,1)}, bf16[16,264,128]{2,1,0:T(8,128)(2,1)S(1)}, u32[]{:S(2)}) copy-start(bf16[16,264,128]{2,1,0:T(8,128)(2,1)S(1)} %all-to-all-done.1.recv.refs_5_) | copy-start | bytes 3244036
  64.3 40.3 %all-to-all-start.2 = ((bf16[16,264,128]{2,1,0:T(8,128)(2,1)}), bf16[16,264,128]{2,1,0:T(8,128)(2,1)S(1)}, u32[]{:S(2)}, u32[]{:S(2)}) async-start(bf16[16,264,128]{2,1,0:T(8,128)(2,1)} %pick.6), calls=%async_computation.2 | async-start | bytes 2162688 | tf_op jit(solution)/shard_map/all_to_all | solution.py:353
  69.1 16.4 %collective-permute-start.5 = (bf16[8,264,128]{2,1,0:T(8,128)(2,1)}, bf16[8,264,128]{2,1,0:T(8,128)(2,1)S(1)}, u32[]{:S(2)}, u32[]{:S(2)}) collective-permute-start(bf16[8,264,128]{2,1,0:T(8,128)(2,1)} %collective-permute-done.3.refs_1_), channel_id=1, source_target_pairs={{0,7},{1,0},{2,1},{3,2},{4,3},{5,4},{6,5},{7,6},{8,15},{9,8},{10,9... | collective-permute-start | bytes 1622024 | tf_op jit(solution)/shard_map/ppermute | solution.py:333
  71.0 17.9 %collective-permute-start.4 = (bf16[8,264,128]{2,1,0:T(8,128)(2,1)}, bf16[8,264,128]{2,1,0:T(8,128)(2,1)S(1)}, u32[]{:S(2)}, u32[]{:S(2)}) collective-permute-start(bf16[8,264,128]{2,1,0:T(8,128)(2,1)} %copy-done.9), channel_id=1, source_target_pairs={{0,1},{1,2},{2,3},{3,4},{4,5},{5,6},{6,7},{7,0},{8,9},{9,10},{10,1... | collective-permute-start | bytes 1622024 | tf_op jit(solution)/shard_map/ppermute | solution.py:333
  85.5 14.4 %copy-start.3 = (bf16[8,264,128]{2,1,0:T(8,128)(2,1)}, bf16[8,264,128]{2,1,0:T(8,128)(2,1)S(1)}, u32[]{:S(2)}) copy-start(bf16[8,264,128]{2,1,0:T(8,128)(2,1)S(1)} %collective-permute-done.5.refs_1_) | copy-start | bytes 1622020
  85.5 9.5 %collective-permute-start.7 = (bf16[4,264,128]{2,1,0:T(8,128)(2,1)S(1)}, bf16[4,264,128]{2,1,0:T(8,128)(2,1)S(1)}, u32[]{:S(2)}, u32[]{:S(2)}) collective-permute-start(bf16[4,264,128]{2,1,0:T(8,128)(2,1)S(1)} %slice.9), channel_id=1, source_target_pairs={{0,7},{1,0},{2,1},{3,2},{4,3},{5,4},{6,5},{7,6},{8,15},{9,8},{10,9... | collective-permute-start | bytes 811016 | tf_op jit(solution)/shard_map/ppermute | solution.py:333
  88.9 10.9 %copy-start.4 = (bf16[8,264,128]{2,1,0:T(8,128)(2,1)}, bf16[8,264,128]{2,1,0:T(8,128)(2,1)S(1)}, u32[]{:S(2)}) copy-start(bf16[8,264,128]{2,1,0:T(8,128)(2,1)S(1)} %collective-permute-done.4.refs_0_) | copy-start | bytes 1622020
  89.0 10.9 %collective-permute-start.6 = (bf16[4,264,128]{2,1,0:T(8,128)(2,1)S(1)}, bf16[4,264,128]{2,1,0:T(8,128)(2,1)}, u32[]{:S(2)}, u32[]{:S(2)}) collective-permute-start(bf16[4,264,128]{2,1,0:T(8,128)(2,1)S(1)} %slice.8), channel_id=1, source_target_pairs={{0,1},{1,2},{2,3},{3,4},{4,5},{5,6},{6,7},{7,0},{8,9},{9,10},{10,1... | collective-permute-start | bytes 811016 | tf_op jit(solution)/shard_map/ppermute | solution.py:333
  95.0 4.8 %copy-start.10 = (bf16[4,264,128]{2,1,0:T(8,128)(2,1)}, bf16[4,264,128]{2,1,0:T(8,128)(2,1)S(1)}, u32[]{:S(2)}) copy-start(bf16[4,264,128]{2,1,0:T(8,128)(2,1)S(1)} %collective-permute-done.7.refs_3_) | copy-start | bytes 811012
  104.6 1.0 copy-start.1
  105.6 26.4 %all-to-all-start.3 = ((bf16[24,264,128]{2,1,0:T(8,128)(2,1)}), bf16[24,264,128]{2,1,0:T(8,128)(2,1)}, u32[]{:S(2)}, u32[]{:S(2)}) async-start(bf16[24,264,128]{2,1,0:T(8,128)(2,1)} %pick.7), calls=%async_computation.3 | async-start | bytes 3244032 | tf_op jit(solution)/shard_map/all_to_all | solution.py:353
where the time goes:
time: 146 us; the launch traced here: 145 us
  Pallas kernels  52.1 us (36%)
  starting transfers between devices  49.9 us (34%)
  waiting for transfers between devices  39.8 us (27%)
  local copies, waits for them, and re-layouts  2.7 us (2%)
    ppermute x8, waiting for transfers between devices, move(): lax.ppermute(what, 'gz', [(z, (z + step) % planes) for z in range(planes)])  39.8 us
    ppermute x8, starting transfers between devices, move(): lax.ppermute(what, 'gz', [(z, (z + step) % planes) for z in range(planes)])  30.4 us
    pallas_call x3, Pallas kernels, render(): pl.pallas_call(render_kernel, name='render', out_shape=jax.ShapeDtypeStru...  21.4 us
    all_to_all x4, starting transfers between devices, spread(): return lax.all_to_all(what, 'gy', split_axis=0, concat_axis=0, tiled=True)  19.5 us
    pallas_call x4, Pallas kernels, pick(): pl.pallas_call(lambda *refs: pick_kernel(parts, *refs), name='pick', out_...  15.4 us
    pallas_call x1, Pallas kernels, body(): pl.pallas_call(paint_kernel, name='paint', out_shape=jax.ShapeDtypeStruct...  12.7 us
  transfers between devices with their start and end apart: 12, of which 7 were waited for; matrix products, arithmetic and copies ran while one was open for 0% of the time, Pallas kernels for 25%

commit v1 on v0

--- a/solution.py
+++ b/solution.py
@@ -47,11 +47,11 @@
     lax.fori_loop(0, bricks.shape[0], one_brick, 0)
 
 
-def pick_kernel(parts, *refs):
+def pick_kernel(parts, *refs, per=None):
     blocks = refs[: len(parts)]
     send, names, names_s, sem = refs[len(parts) :]
     rows = send.shape[1] - META
-    per = 1 + max(place for place, _ in parts)
+    per = per or 1 + max(place for place, _ in parts)
     me = lax.axis_index("gz")
     planes = lax.axis_size("gz")
     start = 0
@@ -87,6 +87,18 @@
         start += block.shape[0]
 
 
+def add_kernel(place, per, block, _, send, fresh, names, names_s, sem, sems):
+    pick_kernel(((0, 0),), block, fresh, names, names_s, sem)
+    copies = [
+        pltpu.make_async_copy(fresh.at[row], send.at[row * per + place], sems.at[row])
+        for row in range(fresh.shape[0])
+    ]
+    for copy in copies:
+        copy.start()
+    for copy in copies:
+        copy.wait()
+
+
 def as_row(column, count, empty=0.0):
     lane = lax.broadcasted_iota(jnp.int32, (count, 128), 1)
     line = lax.broadcasted_iota(jnp.int32, (count, 128), 0)
@@ -106,38 +118,48 @@
     return jnp.sum(jnp.where(hit, line, 0.0), axis=0, keepdims=True)
 
 
-def plan(meta, first, ints, reals):
+def field_of(meta, at):
+    lane = lax.broadcasted_iota(jnp.int32, meta.shape, 1)
+    return jnp.sum(jnp.where(lane == at, meta, 0.0), axis=1, keepdims=True)
+
+
+def total_of(mask):
+    zero = jnp.zeros((1, 128), F32)
+    return zero + jnp.sum(jnp.where(mask, 1.0, 0.0), axis=0, keepdims=True)
+
+
+def index_of(meta):
+    return lax.broadcasted_iota(jnp.int32, (meta.shape[0], 1), 0).astype(F32)
+
+
+def plan_draw(meta, ints, reals):
     count = meta.shape[0]
-    lane = lax.broadcasted_iota(jnp.int32, (count, 128), 1)
-    index = lax.broadcasted_iota(jnp.int32, (count, 1), 0).astype(F32)
-
-    def field(at):
-        return jnp.sum(jnp.where(lane == at, meta, 0.0), axis=1, keepdims=True)
-
-    def total(mask):
-        zero = jnp.zeros((1, 128), F32)
-        return zero + jnp.sum(jnp.where(mask, 1.0, 0.0), axis=0, keepdims=True)
-
-    tile_1 = field(0)
-    rank = field(1) * 64.0 + field(2)
-    live = field(5)
+    tile_1 = field_of(meta, 0)
+    live = field_of(meta, 5)
     valid = tile_1 > 0.5
-    fresh = valid & (index > first - 0.5)
-    by_live = jnp.where(fresh, live * 256.0 + index, 4096.0 + index)
-    by_rank = jnp.where(valid, tile_1 * 4096.0 + rank, 16384.0 + index)
+    index = index_of(meta)
+    key = jnp.where(valid, live * 256.0 + index, 4096.0 + index)
     rows = (
-        order_of(by_live, count),
-        order_of(by_rank, count),
-        total(fresh & (live < 1.5)),
-        total(fresh),
-        total(valid),
-        total(valid & (tile_1 < 1.5)),
+        order_of(key, count),
+        total_of(valid & (live < 1.5)),
+        total_of(valid),
         as_row(tile_1, count),
     )
     for at, row in enumerate(rows):
         ints[at : at + 1, :] = row.astype(jnp.int32)
-    for at, row in enumerate((field(3), field(4), field(6))):
-        reals[at : at + 1, :] = as_row(row, count)
+    for at, name in enumerate((3, 4, 6)):
+        reals[at : at + 1, :] = as_row(field_of(meta, name), count)
+
+
+def plan_lay(meta, ints):
+    count = meta.shape[0]
+    tile_1 = field_of(meta, 0)
+    rank = field_of(meta, 1) * 64.0 + field_of(meta, 2)
+    valid = tile_1 > 0.5
+    key = jnp.where(valid, tile_1 * 4096.0 + rank, 16384.0 + index_of(meta))
+    rows = (order_of(key, count), total_of(valid & (tile_1 < 1.5)), total_of(valid))
+    for at, row in enumerate(rows):
+        ints[at : at + 1, :] = row.astype(jnp.int32)
 
 
 def draw_all(shear, gain, bias, recv, first, feet, bufs, ints_s, reals_s):
@@ -152,13 +174,13 @@
     biases = [0.5 * bias[c] for c in range(3)]
 
     def density(slot, layer, out):
-        view = view_base + ints_s[6, slot] - 1
+        view = view_base + ints_s[3, slot] - 1
         raised = F32(layer - layers // 2)
         sx = reals_s[0, slot] + raised * shear[0, view]
         sy = reals_s[1, slot] + raised * shear[1, view]
         across = jnp.maximum(0.0, 1.0 - jnp.abs(apart - sx)).astype(BF16)
         downward = jnp.maximum(0.0, 1.0 - jnp.abs(apart + sy)).astype(BF16)
-        source = recv[slot - first, layer * extent : (layer + 1) * extent, :]
+        source = recv[slot, layer * extent : (layer + 1) * extent, :]
         halfway = jnp.dot(across, source, preferred_element_type=F32).astype(BF16)
         out[...] = jnp.dot(halfway, downward, preferred_element_type=F32)
 
@@ -183,8 +205,8 @@
                     now = half * jnp.tanh(gains[c] * d + biases[c]) + half
                     colors[c] = now if colors[c] is None else colors[c] + now
             for c in range(3):
-                feet[slot, c, span, :] = colors[c].astype(BF16)
-            feet[slot, 3, span, :] = optical.astype(BF16)
+                feet[first + slot, c, span, :] = colors[c].astype(BF16)
+            feet[first + slot, 3, span, :] = optical.astype(BF16)
 
     def render(begin, end, layer_count, bufs_a, bufs_b):
         def fill(at, dens):
@@ -209,8 +231,8 @@
 
             lax.fori_loop(0, lax.div(end - begin + 1, 2), two, 0)
 
-    short_n = ints_s[2, 0]
-    fresh_n = ints_s[3, 0]
+    short_n = ints_s[1, 0]
+    fresh_n = ints_s[2, 0]
     render(0, short_n, 1, bufs[0:1], bufs[2:3])
     render(short_n, fresh_n, 2, bufs[0:2], bufs[2:4])
 
@@ -218,7 +240,7 @@
 def render_kernel(shear, gain, bias, recv, feet, b0, b1, b2, b3, ints, reals, ints_s, reals_s, sems):
     rows = recv.shape[1] - META
     meta = jnp.max(recv[:, rows : rows + META, :].astype(F32), axis=1)
-    plan(meta, 0, ints, reals)
+    plan_draw(meta, ints, reals)
     copies = [
         pltpu.make_async_copy(ints, ints_s, sems.at[0]),
         pltpu.make_async_copy(reals, reals_s, sems.at[1]),
@@ -232,53 +254,57 @@
 
 def paint_kernel(*refs):
     shear, gain, bias = refs[:3]
-    (image, feet, b0, b1, b2, b3, lines, ints, reals, ints_s, reals_s, sems) = refs[-12:]
-    middle = refs[3:-12]
-    recv = middle[-1]
+    (image, feet, b0, b1, b2, b3, lines, recv, places, places_s) = refs[-15:-5]
+    (ints, reals, ints_s, reals_s, sems) = refs[-5:]
+    middle = refs[3:-15]
+    last = middle[-1]
     done = len(middle) // 2
-    extent = recv.shape[2]
-    rows = recv.shape[1] - META
+    extent = last.shape[2]
+    rows = last.shape[1] - META
+    meta_copies, feet_copies = [], []
     first = 0
-    meta_copies, feet_copies = [], []
-    for group in range(done):
-        old, old_feet = middle[2 * group], middle[2 * group + 1]
-        count = old.shape[0]
-        span = pl.ds(first, count)
+    for group in range(done + 1):
+        old = middle[2 * group]
+        span = pl.ds(first, old.shape[0])
         meta_copies.append(
             pltpu.make_async_copy(
-                old.at[:, pl.ds(rows, META), :], lines.at[span], sems.at[2 * group + 2]
+                old.at[:, pl.ds(rows, META), :], lines.at[span], sems.at[2 * group]
             )
         )
-        feet_copies.append(
-            pltpu.make_async_copy(old_feet, feet.at[span], sems.at[2 * group + 3])
-        )
-        first += count
-    for copy in meta_copies + feet_copies:
+        if group < done:
+            feet_copies.append(
+                pltpu.make_async_copy(middle[2 * group + 1], feet.at[span], sems.at[2 * group + 1])
+            )
+            first += old.shape[0]
+    bulk = pltpu.make_async_copy(last, recv, sems.at[2 * done + 1])
+    for copy in meta_copies[::-1] + [bulk] + feet_copies:
         copy.start()
-    lines[first : first + recv.shape[0]] = recv[:, rows : rows + META, :]
+    draw_ints = pltpu.make_async_copy(ints, ints_s, sems.at[2 * done + 2])
+    draw_reals = pltpu.make_async_copy(reals, reals_s, sems.at[2 * done + 3])
+    lay_ints = pltpu.make_async_copy(places, places_s, sems.at[2 * done + 4])
     image[...] = jnp.zeros_like(image)
-    for copy in meta_copies:
+    meta_copies[-1].wait()
+    plan_draw(jnp.max(lines[first:].astype(F32), axis=1), ints, reals)
+    draw_ints.start()
+    draw_reals.start()
+    for copy in meta_copies[:-1]:
         copy.wait()
-    meta = jnp.max(lines[...].astype(F32), axis=1)
-    plan(meta, first, ints, reals)
-    copies = [
-        pltpu.make_async_copy(ints, ints_s, sems.at[0]),
-        pltpu.make_async_copy(reals, reals_s, sems.at[1]),
-    ]
-    for copy in copies:
-        copy.start()
-    for copy in copies:
-        copy.wait()
+    plan_lay(jnp.max(lines[...].astype(F32), axis=1), places)
+    lay_ints.start()
+    draw_ints.wait()
+    draw_reals.wait()
+    bulk.wait()
     draw_all(shear, gain, bias, recv, first, feet, (b0, b1, b2, b3), ints_s, reals_s)
     for copy in feet_copies:
         copy.wait()
-
-    all_n = ints_s[4, 0]
-    first_n = ints_s[5, 0]
+    lay_ints.wait()
+
+    all_n = places_s[2, 0]
+    first_n = places_s[1, 0]
     for tile in range(2):
 
         def lay(at, _):
-            slot = ints_s[1, at]
+            slot = places_s[0, at]
             for begin in range(0, extent, PART):
                 span = slice(begin, begin + PART)
                 optical = image[tile, 3, span, :]
@@ -332,11 +358,11 @@
     def move(what, step):
         return lax.ppermute(what, "gz", [(z, (z + step) % planes) for z in range(planes)])
 
-    def pick(parts, blocks):
-        per = 1 + max(place for place, _ in parts)
+    def pick(parts, blocks, per=None):
+        per = per or 1 + max(place for place, _ in parts)
         total = sum(b.shape[0] for b in blocks)
         return pl.pallas_call(
-            lambda *refs: pick_kernel(parts, *refs),
+            lambda *refs: pick_kernel(parts, *refs, per=per),
             name="pick",
             out_shape=jax.ShapeDtypeStruct((columns * per, rows + META, extent), BF16),
             in_specs=[vmem] * len(blocks),
@@ -349,6 +375,24 @@
             cost_estimate=pl.CostEstimate(flops=0, bytes_accessed=6_000_000, transcendentals=0),
         )(*blocks)
 
+    def add(send, place, block):
+        per = send.shape[0] // columns
+        return pl.pallas_call(
+            lambda *refs: add_kernel(place, per, *refs),
+            name="add",
+            out_shape=jax.ShapeDtypeStruct(send.shape, BF16),
+            in_specs=[vmem, here],
+            out_specs=here,
+            input_output_aliases={1: 0},
+            scratch_shapes=[
+                VMEM((columns, rows + META, extent), BF16),
+                VMEM((count, 128), jnp.int32),
+                SMEM((count, 128), jnp.int32),
+                pltpu.SemaphoreType.DMA,
+                pltpu.SemaphoreType.DMA((columns,)),
+            ],
+        )(block, send)
+
     def spread(what):
         return lax.all_to_all(what, "gy", split_axis=0, concat_axis=0, tiled=True)
 
@@ -361,26 +405,27 @@
             in_specs=[smem] * 3 + [vmem],
             out_specs=vmem,
             scratch_shapes=tables + small + [pltpu.SemaphoreType.DMA((2,))],
+            compiler_params=pltpu.CompilerParams(vmem_limit_bytes=67_043_328),
             cost_estimate=pl.CostEstimate(flops=0, bytes_accessed=8_000_000, transcendentals=0),
         )(shear.T, color_gain, color_bias, recv)
 
-    half = count // 2
     ups, downs = [block], [block]
     for _ in range(1, planes // 2):
         ups.append(move(ups[-1], 1))
         downs.append(move(downs[-1], -1))
-    up_far = move(ups[-1][:half], 1)
-    down_far = move(downs[-1][half:], -1)
+    far = move(ups[-1], 1)
 
     groups = (
         (((0, 0),), (block,)),
         (((0, 0), (1, 0)), (ups[1], downs[1])),
         (((0, 0), (1, 0)), (ups[2], downs[2])),
-        (((0, 0), (1, 0), (2, 0), (2, 0)), (ups[3], downs[3], up_far, down_far)),
+        (((0, 0), (1, 0)), (ups[3], downs[3])),
     )
     received = []
-    for parts, blocks in groups:
-        send = pick(parts, blocks)
+    for at, (parts, blocks) in enumerate(groups):
+        send = pick(parts, blocks, 3 if at == 3 else None)
+        if at == 3:
+            send = add(send, 2, far)
         received.append(spread(send))
     slots = sum(r.shape[0] for r in received)
     middle = []
@@ -390,13 +435,18 @@
         paint_kernel,
         name="paint",
         out_shape=jax.ShapeDtypeStruct((2, 4, extent, extent), F32),
-        in_specs=[smem] * 3 + [here] * len(middle) + [vmem],
+        in_specs=[smem] * 3 + [here] * (len(middle) + 1),
         out_specs=vmem,
         scratch_shapes=[VMEM((slots, 4, extent, extent), BF16)]
         + tables
-        + [VMEM((slots, META, 128), BF16)]
+        + [
+            VMEM((slots, META, 128), BF16),
+            VMEM(received[-1].shape, BF16),
+            VMEM((8, 128), jnp.int32),
+            SMEM((8, 128), jnp.int32),
+        ]
         + small
-        + [pltpu.SemaphoreType.DMA((2 + len(middle),))],
+        + [pltpu.SemaphoreType.DMA((5 + len(middle),))],
     )(shear.T, color_gain, color_bias, *middle, received[-1])
 
 

time: 146 us -> 135 us (0.925)
  waiting for transfers between devices: 39.8 us -> 29.1 us
  starting transfers between devices: 49.9 us -> 48.1 us
  Pallas kernels: 52.1 us -> 53.6 us
    ppermute x8 -> x7, waiting for transfers between devices: 39.8 us -> 29.1 us  [move(): lax.ppermute(what, 'gz', [(z, (z + step) % planes) for z in range(planes)])]
    pallas_call x4 -> x5, Pallas kernels: 15.4 us -> 17.7 us  [the longest x4 14.6 us: pick(): pl.pallas_call(lambda *refs: pick_kernel(parts, *refs, per=per), name='pi...]
    ppermute x8 -> x7, starting transfers between devices: 30.4 us -> 28.8 us  [move(): lax.ppermute(what, 'gz', [(z, (z + step) % planes) for z in range(planes)])]
    unnamed x22 -> x20, local copies, waits for them, and re-layouts: 2.66 us -> 3.49 us
  transfers between devices with their start and end apart: 12 -> 11, of which waited for: 7 -> 5; matrix products, arithmetic and copies ran while one was open for 0% -> 0% of each run, Pallas kernels for 25% -> 29%
where the time goes in v1:
time: 135 us
  Pallas kernels  53.6 us (40%)
  starting transfers between devices  48.1 us (36%)
  waiting for transfers between devices  29.1 us (22%)
  local copies, waits for them, and re-layouts  3.49 us (3%)
    ppermute x7, waiting for transfers between devices, move(): lax.ppermute(what, 'gz', [(z, (z + step) % planes) for z in range(planes)])  29.1 us
    ppermute x7, starting transfers between devices, move(): lax.ppermute(what, 'gz', [(z, (z + step) % planes) for z in range(planes)])  28.8 us
    pallas_call x3, Pallas kernels, render(): pl.pallas_call(render_kernel, name='render', out_shape=jax.ShapeDtypeStru...  21.4 us
    all_to_all x4, starting transfers between devices, spread(): return lax.all_to_all(what, 'gy', split_axis=0, concat_axis=0, tiled=True)  19.2 us
    pallas_call x4, Pallas kernels, pick(): pl.pallas_call(lambda *refs: pick_kernel(parts, *refs, per=per), name='pi...  14.6 us
    pallas_call x1, Pallas kernels, body(): pl.pallas_call(paint_kernel, name='paint', out_shape=jax.ShapeDtypeStruct...  11.9 us
    unnamed x20, local copies, waits for them, and re-layouts  3.49 us
    pallas_call x1, Pallas kernels, add(): pl.pallas_call(lambda *refs: add_kernel(place, per, *refs), name='add', o...  3.06 us
  transfers between devices with their start and end apart: 11, of which 5 were waited for; matrix products, arithmetic and copies ran while one was open for 0% of the time, Pallas kernels for 29%

profile of v1, /device:TPU:38, one launch (start us, length us, event | category | flops | bytes accessed | tf_op | source)
XLA Modules:
  0.0 134.5 jit_solution(6065206694171582668)
XLA Ops:
  0.0 2.6 %label.1.refs_0_ = bf16[8,264,128]{2,1,0:T(8,128)(2,1)} custom-call(s32[4,8]{1,0:T(4,128)} %bitcast.11, s32[4,8]{1,0:T(4,128)} %order.1, s32[4,2,8]{2,1,0:T(2,128)} %bitcast.10, s32[8]{0:T(128)} %live.1, bf16[1,8]{1,0:T(2,128)(2,1)} %bitcast.12, bf16[8,256,128]{2,1,0:T(8,128)(2,1)} %bitcast.5), custom_call_target="tpu_custom_call" | custom-call | tf_op jit(solution)/shard_map/label/pallas_call | solution.py:343
  2.6 10.9 %collective-permute-start.1 = (bf16[8,264,128]{2,1,0:T(8,128)(2,1)}, bf16[8,264,128]{2,1,0:T(8,128)(2,1)S(1)}, u32[]{:S(2)}, u32[]{:S(2)}) collective-permute-start(bf16[8,264,128]{2,1,0:T(8,128)(2,1)} %label.1.refs_0_), channel_id=1, source_target_pairs={{0,7},{1,0},{2,1},{3,2},{4,3},{5,4},{6,5},{7,6},{8,15},{9,8},{10,9... | collective-permute-start | bytes 1622024 | tf_op jit(solution)/shard_map/ppermute | solution.py:359
  13.6 1.9 %collective-permute-start = (bf16[8,264,128]{2,1,0:T(8,128)(2,1)}, bf16[8,264,128]{2,1,0:T(8,128)(2,1)S(1)}, u32[]{:S(2)}, u32[]{:S(2)}) collective-permute-start(bf16[8,264,128]{2,1,0:T(8,128)(2,1)} %label.1.refs_0_), channel_id=1, source_target_pairs={{0,1},{1,2},{2,3},{3,4},{4,5},{5,6},{6,7},{7,0},{8,9},{9,10},{10,1... | collective-permute-start | bytes 1622024 | tf_op jit(solution)/shard_map/ppermute | solution.py:359
  15.5 2.9 %pick.4 = bf16[8,264,128]{2,1,0:T(8,128)(2,1)} custom-call(bf16[8,264,128]{2,1,0:T(8,128)(2,1)} %label.1.refs_0_), custom_call_target="tpu_custom_call" | custom-call | bytes 6000000 | tf_op jit(solution)/shard_map/pick/pallas_call | solution.py:364
  18.5 4.8 %all-to-all-start = ((bf16[8,264,128]{2,1,0:T(8,128)(2,1)}), bf16[8,264,128]{2,1,0:T(8,128)(2,1)S(1)}, u32[]{:S(2)}, u32[]{:S(2)}) async-start(bf16[8,264,128]{2,1,0:T(8,128)(2,1)} %pick.4), calls=%async_computation | async-start | bytes 1081344 | tf_op jit(solution)/shard_map/all_to_all | solution.py:397
  23.2 2.2 %collective-permute-done.1.refs_1_ = bf16[8,264,128]{2,1,0:T(8,128)(2,1)S(1)} collective-permute-done((bf16[8,264,128]{2,1,0:T(8,128)(2,1)}, bf16[8,264,128]{2,1,0:T(8,128)(2,1)S(1)}, u32[]{:S(2)}, u32[]{:S(2)}) %collective-permute-start.1) | collective-permute-done | bytes 540704 | tf_op jit(solution)/shard_map/ppermute | solution.py:359
  25.4 0.0 copy-start.3
  25.4 5.2 %collective-permute-done.refs_0_ = bf16[8,264,128]{2,1,0:T(8,128)(2,1)S(1)} collective-permute-done((bf16[8,264,128]{2,1,0:T(8,128)(2,1)}, bf16[8,264,128]{2,1,0:T(8,128)(2,1)S(1)}, u32[]{:S(2)}, u32[]{:S(2)}) %collective-permute-start) | collective-permute-done | bytes 540704 | tf_op jit(solution)/shard_map/ppermute | solution.py:359
  30.6 0.0 copy-done.3
  30.6 0.0 copy-start.8
  30.6 0.8 copy-done.8
  31.4 3.8 %pick.5 = bf16[16,264,128]{2,1,0:T(8,128)(2,1)} custom-call(bf16[8,264,128]{2,1,0:T(8,128)(2,1)} %copy-done.8, bf16[8,264,128]{2,1,0:T(8,128)(2,1)} %copy-done.3), custom_call_target="tpu_custom_call" | custom-call | bytes 6000000 | tf_op jit(solution)/shard_map/pick/pallas_call | solution.py:364
  35.3 0.0 copy-start.9
  35.3 0.0 copy-start.4
  35.3 0.0 all-to-all-done.recv.refs_3_
  35.3 0.0 copy-start.2
  35.3 0.8 copy-done.2
  36.1 4.7 %all-to-all-start.1 = ((bf16[16,264,128]{2,1,0:T(8,128)(2,1)}), bf16[16,264,128]{2,1,0:T(8,128)(2,1)S(1)}, u32[]{:S(2)}, u32[]{:S(2)}) async-start(bf16[16,264,128]{2,1,0:T(8,128)(2,1)} %pick.5), calls=%async_computation.1 | async-start | bytes 2162688 | tf_op jit(solution)/shard_map/all_to_all | solution.py:397
  40.9 0.0 copy-done.9
  40.9 1.9 %collective-permute-start.2 = (bf16[8,264,128]{2,1,0:T(8,128)(2,1)S(1)}, bf16[8,264,128]{2,1,0:T(8,128)(2,1)}, u32[]{:S(2)}, u32[]{:S(2)}) collective-permute-start(bf16[8,264,128]{2,1,0:T(8,128)(2,1)S(1)} %copy-done.9), channel_id=1, source_target_pairs={{0,1},{1,2},{2,3},{3,4},{4,5},{5,6},{6,7},{7,0},{8,9},{9,10},{10,1... | collective-permute-start | bytes 1622024 | tf_op jit(solution)/shard_map/ppermute | solution.py:359
  42.8 0.0 copy-done.4
  42.8 5.1 %collective-permute-start.3 = (bf16[8,264,128]{2,1,0:T(8,128)(2,1)S(1)}, bf16[8,264,128]{2,1,0:T(8,128)(2,1)S(1)}, u32[]{:S(2)}, u32[]{:S(2)}) collective-permute-start(bf16[8,264,128]{2,1,0:T(8,128)(2,1)S(1)} %copy-done.4), channel_id=1, source_target_pairs={{0,7},{1,0},{2,1},{3,2},{4,3},{5,4},{6,5},{7,6},{8,15},{9,8},{10,9... | collective-permute-start | bytes 1622024 | tf_op jit(solution)/shard_map/ppermute | solution.py:359
  47.9 10.4 %collective-permute-done.2.refs_0_ = bf16[8,264,128]{2,1,0:T(8,128)(2,1)} collective-permute-done((bf16[8,264,128]{2,1,0:T(8,128)(2,1)S(1)}, bf16[8,264,128]{2,1,0:T(8,128)(2,1)}, u32[]{:S(2)}, u32[]{:S(2)}) %collective-permute-start.2) | collective-permute-done | bytes 540704 | tf_op jit(solution)/shard_map/ppermute | solution.py:359
  58.4 1.9 %collective-permute-start.4 = (bf16[8,264,128]{2,1,0:T(8,128)(2,1)}, bf16[8,264,128]{2,1,0:T(8,128)(2,1)S(1)}, u32[]{:S(2)}, u32[]{:S(2)}) collective-permute-start(bf16[8,264,128]{2,1,0:T(8,128)(2,1)} %collective-permute-done.2.refs_0_), channel_id=1, source_target_pairs={{0,1},{1,2},{2,3},{3,4},{4,5},{5,6},{6,7},{7,0},{8,9},{9,10},{10,1... | collective-permute-start | bytes 1622024 | tf_op jit(solution)/shard_map/ppermute | solution.py:359
  60.3 0.0 collective-permute-done.3.refs_1_
  60.3 0.0 copy-start.5
  60.3 0.8 copy-done.5
  61.1 3.9 %pick.6 = bf16[16,264,128]{2,1,0:T(8,128)(2,1)} custom-call(bf16[8,264,128]{2,1,0:T(8,128)(2,1)} %collective-permute-done.2.refs_0_, bf16[8,264,128]{2,1,0:T(8,128)(2,1)} %copy-done.5), custom_call_target="tpu_custom_call" | custom-call | bytes 6000000 | tf_op jit(solution)/shard_map/pick/pallas_call | solution.py:364
  65.0 0.0 copy-start.6
  65.0 0.0 all-to-all-done.1.recv.refs_5_
  65.0 0.0 copy-start
  65.0 5.0 %all-to-all-start.2 = ((bf16[16,264,128]{2,1,0:T(8,128)(2,1)}), bf16[16,264,128]{2,1,0:T(8,128)(2,1)S(1)}, u32[]{:S(2)}, u32[]{:S(2)}) async-start(bf16[16,264,128]{2,1,0:T(8,128)(2,1)} %pick.6), calls=%async_computation.2 | async-start | bytes 2162688 | tf_op jit(solution)/shard_map/all_to_all | solution.py:397
  70.0 0.0 copy-done.6
  70.0 5.1 %collective-permute-start.6 = (bf16[8,264,128]{2,1,0:T(8,128)(2,1)S(1)}, bf16[8,264,128]{2,1,0:T(8,128)(2,1)}, u32[]{:S(2)}, u32[]{:S(2)}) collective-permute-start(bf16[8,264,128]{2,1,0:T(8,128)(2,1)S(1)} %copy-done.6), channel_id=1, source_target_pairs={{0,7},{1,0},{2,1},{3,2},{4,3},{5,4},{6,5},{7,6},{8,15},{9,8},{10,9... | collective-permute-start | bytes 1622024 | tf_op jit(solution)/shard_map/ppermute | solution.py:359
  75.1 0.0 collective-permute-done.4.refs_0_
  75.1 0.0 copy-start.7
  75.1 1.9 %collective-permute-start.5 = (bf16[8,264,128]{2,1,0:T(8,128)(2,1)S(1)}, bf16[8,264,128]{2,1,0:T(8,128)(2,1)}, u32[]{:S(2)}, u32[]{:S(2)}) collective-permute-start(bf16[8,264,128]{2,1,0:T(8,128)(2,1)S(1)} %collective-permute-done.4.refs_0_), channel_id=1, source_target_pairs={{0,1},{1,2},{2,3},{3,4},{4,5},{5,6},{6,7},{7,0},{8,9},{9,10},{10,1... | collective-permute-start | bytes 1622024 | tf_op jit(solution)/shard_map/ppermute | solution.py:359
  77.0 9.8 %collective-permute-done.6.refs_1_ = bf16[8,264,128]{2,1,0:T(8,128)(2,1)} collective-permute-done((bf16[8,264,128]{2,1,0:T(8,128)(2,1)S(1)}, bf16[8,264,128]{2,1,0:T(8,128)(2,1)}, u32[]{:S(2)}, u32[]{:S(2)}) %collective-permute-start.6) | collective-permute-done | bytes 540704 | tf_op jit(solution)/shard_map/ppermute | solution.py:359
  86.9 0.0 copy-done.7
  86.9 4.0 %pick.7.refs_1_ = bf16[24,264,128]{2,1,0:T(8,128)(2,1)} custom-call(bf16[8,264,128]{2,1,0:T(8,128)(2,1)} %copy-done.7, bf16[8,264,128]{2,1,0:T(8,128)(2,1)} %collective-permute-done.6.refs_1_), custom_call_target="tpu_custom_call" | custom-call | bytes 6000000 | tf_op jit(solution)/shard_map/pick/pallas_call | solution.py:364
  90.9 0.0 copy-done
  90.9 1.4 %collective-permute-done.5.refs_0_ = bf16[8,264,128]{2,1,0:T(8,128)(2,1)} collective-permute-done((bf16[8,264,128]{2,1,0:T(8,128)(2,1)S(1)}, bf16[8,264,128]{2,1,0:T(8,128)(2,1)}, u32[]{:S(2)}, u32[]{:S(2)}) %collective-permute-start.5) | collective-permute-done | bytes 540704 | tf_op jit(solution)/shard_map/ppermute | solution.py:359
  92.3 3.1 %add.1 = bf16[24,264,128]{2,1,0:T(8,128)(2,1)} custom-call(bf16[8,264,128]{2,1,0:T(8,128)(2,1)} %collective-permute-done.5.refs_0_, bf16[24,264,128]{2,1,0:T(8,128)(2,1)} %pick.7.refs_1_), custom_call_target="tpu_custom_call", output_to_operand_aliasing={{}: (1, {})} | custom-call | tf_op jit(solution)/shard_map/add/pallas_call | solution.py:380
  95.4 0.0 all-to-all-done.2.recv.refs_7_
  95.4 0.0 copy-start.1
  95.4 1.1 copy-done.1
  96.5 4.8 %all-to-all-start.3 = ((bf16[24,264,128]{2,1,0:T(8,128)(2,1)}), bf16[24,264,128]{2,1,0:T(8,128)(2,1)}, u32[]{:S(2)}, u32[]{:S(2)}) async-start(bf16[24,264,128]{2,1,0:T(8,128)(2,1)} %add.1), calls=%async_computation.3 | async-start | bytes 3244032 | tf_op jit(solution)/shard_map/all_to_all | solution.py:397
  101.2 5.7 %render.3.refs_4_ = bf16[8,4,128,128]{3,2,1,0:T(8,128)(2,1)} custom-call(f32[2,4]{1,0:T(2,128)} %bitcast.6, f32[3]{0:T(128)} %refs_1_.1, f32[3]{0:T(128)} %refs_2_.1, bf16[8,264,128]{2,1,0:T(8,128)(2,1)} %copy-done.2), custom_call_target="tpu_custom_call" | custom-call | bytes 8000000 | tf_op jit(solution)/shard_map/render/pallas_call | solution.py:401
  107.0 7.9 %render.4.refs_6_ = bf16[16,4,128,128]{3,2,1,0:T(8,128)(2,1)} custom-call(f32[2,4]{1,0:T(2,128)} %bitcast.7, f32[3]{0:T(128)} %refs_1_.1, f32[3]{0:T(128)} %refs_2_.1, bf16[16,264,128]{2,1,0:T(8,128)(2,1)} %copy-done), custom_call_target="tpu_custom_call" | custom-call | bytes 8000000 | tf_op jit(solution)/shard_map/render/pallas_call | solution.py:401
  114.9 7.7 %render.5.refs_8_ = bf16[16,4,128,128]{3,2,1,0:T(8,128)(2,1)} custom-call(f32[2,4]{1,0:T(2,128)} %bitcast.8, f32[3]{0:T(128)} %refs_1_.1, f32[3]{0:T(128)} %refs_2_.1, bf16[16,264,128]{2,1,0:T(8,128)(2,1)} %copy-done.1), custom_call_target="tpu_custom_call" | custom-call | bytes 8000000 | tf_op jit(solution)/shard_map/render/pallas_call | solution.py:401
  122.7 0.0 all-to-all-done.3.refs_9_
  122.7 11.9 %paint.1 = f32[2,4,128,128]{3,2,1,0:T(8,128)} custom-call(f32[2,4]{1,0:T(2,128)} %bitcast.9, f32[3]{0:T(128)} %refs_1_.1, f32[3]{0:T(128)} %refs_2_.1, bf16[8,264,128]{2,1,0:T(8,128)(2,1)} %copy-done.2, bf16[8,4,128,128]{3,2,1,0:T(8,128)(2,1)} %render.3.refs_4_, bf16[16,264,128]{2,1,0:T(8,128)(2,1)} %copy-done, bf16[16,4,128,128]{3,2,1,0:T(8,128)(2,1)} %render.4.refs_6_, ...), custom_call_target="tpu_custom_call" | custom-call | tf_op jit(solution)/shard_map/paint/pallas_call | solution.py:434
Async XLA Ops:
  2.6 22.8 %collective-permute-start.1 = (bf16[8,264,128]{2,1,0:T(8,128)(2,1)}, bf16[8,264,128]{2,1,0:T(8,128)(2,1)S(1)}, u32[]{:S(2)}, u32[]{:S(2)}) collective-permute-start(bf16[8,264,128]{2,1,0:T(8,128)(2,1)} %label.1.refs_0_), channel_id=1, source_target_pairs={{0,7},{1,0},{2,1},{3,2},{4,3},{5,4},{6,5},{7,6},{8,15},{9,8},{10,9... | collective-permute-start | bytes 1622024 | tf_op jit(solution)/shard_map/ppermute | solution.py:359
  13.6 17.0 %collective-permute-start = (bf16[8,264,128]{2,1,0:T(8,128)(2,1)}, bf16[8,264,128]{2,1,0:T(8,128)(2,1)S(1)}, u32[]{:S(2)}, u32[]{:S(2)}) collective-permute-start(bf16[8,264,128]{2,1,0:T(8,128)(2,1)} %label.1.refs_0_), channel_id=1, source_target_pairs={{0,1},{1,2},{2,3},{3,4},{4,5},{5,6},{6,7},{7,0},{8,9},{9,10},{10,1... | collective-permute-start | bytes 1622024 | tf_op jit(solution)/shard_map/ppermute | solution.py:359
  18.5 16.9 %all-to-all-start = ((bf16[8,264,128]{2,1,0:T(8,128)(2,1)}), bf16[8,264,128]{2,1,0:T(8,128)(2,1)S(1)}, u32[]{:S(2)}, u32[]{:S(2)}) async-start(bf16[8,264,128]{2,1,0:T(8,128)(2,1)} %pick.4), calls=%async_computation | async-start | bytes 1081344 | tf_op jit(solution)/shard_map/all_to_all | solution.py:397
  25.4 5.2 %copy-start.3 = (bf16[8,264,128]{2,1,0:T(8,128)(2,1)}, bf16[8,264,128]{2,1,0:T(8,128)(2,1)S(1)}, u32[]{:S(2)}) copy-start(bf16[8,264,128]{2,1,0:T(8,128)(2,1)S(1)} %collective-permute-done.1.refs_1_) | copy-start | bytes 1622020
  30.6 0.8 copy-start.8
  35.3 5.6 %copy-start.9 = (bf16[8,264,128]{2,1,0:T(8,128)(2,1)S(1)}, bf16[8,264,128]{2,1,0:T(8,128)(2,1)}, u32[]{:S(2)}) copy-start(bf16[8,264,128]{2,1,0:T(8,128)(2,1)} %copy-done.8) | copy-start | bytes 1622020
  35.3 7.5 %copy-start.4 = (bf16[8,264,128]{2,1,0:T(8,128)(2,1)S(1)}, bf16[8,264,128]{2,1,0:T(8,128)(2,1)}, u32[]{:S(2)}) copy-start(bf16[8,264,128]{2,1,0:T(8,128)(2,1)} %copy-done.3) | copy-start | bytes 1622020
  35.3 0.8 copy-start.2
  36.1 28.8 %all-to-all-start.1 = ((bf16[16,264,128]{2,1,0:T(8,128)(2,1)}), bf16[16,264,128]{2,1,0:T(8,128)(2,1)S(1)}, u32[]{:S(2)}, u32[]{:S(2)}) async-start(bf16[16,264,128]{2,1,0:T(8,128)(2,1)} %pick.5), calls=%async_computation.1 | async-start | bytes 2162688 | tf_op jit(solution)/shard_map/all_to_all | solution.py:397
  40.9 17.5 %collective-permute-start.2 = (bf16[8,264,128]{2,1,0:T(8,128)(2,1)S(1)}, bf16[8,264,128]{2,1,0:T(8,128)(2,1)}, u32[]{:S(2)}, u32[]{:S(2)}) collective-permute-start(bf16[8,264,128]{2,1,0:T(8,128)(2,1)S(1)} %copy-done.9), channel_id=1, source_target_pairs={{0,1},{1,2},{2,3},{3,4},{4,5},{5,6},{6,7},{7,0},{8,9},{9,10},{10,1... | collective-permute-start | bytes 1622024 | tf_op jit(solution)/shard_map/ppermute | solution.py:359
  42.8 17.5 %collective-permute-start.3 = (bf16[8,264,128]{2,1,0:T(8,128)(2,1)S(1)}, bf16[8,264,128]{2,1,0:T(8,128)(2,1)S(1)}, u32[]{:S(2)}, u32[]{:S(2)}) collective-permute-start(bf16[8,264,128]{2,1,0:T(8,128)(2,1)S(1)} %copy-done.4), channel_id=1, source_target_pairs={{0,7},{1,0},{2,1},{3,2},{4,3},{5,4},{6,5},{7,6},{8,15},{9,8},{10,9... | collective-permute-start | bytes 1622024 | tf_op jit(solution)/shard_map/ppermute | solution.py:359
  58.4 16.7 %collective-permute-start.4 = (bf16[8,264,128]{2,1,0:T(8,128)(2,1)}, bf16[8,264,128]{2,1,0:T(8,128)(2,1)S(1)}, u32[]{:S(2)}, u32[]{:S(2)}) collective-permute-start(bf16[8,264,128]{2,1,0:T(8,128)(2,1)} %collective-permute-done.2.refs_0_), channel_id=1, source_target_pairs={{0,1},{1,2},{2,3},{3,4},{4,5},{5,6},{6,7},{7,0},{8,9},{9,10},{10,1... | collective-permute-start | bytes 1622024 | tf_op jit(solution)/shard_map/ppermute | solution.py:359
  60.3 0.8 copy-start.5
  65.0 5.0 %copy-start.6 = (bf16[8,264,128]{2,1,0:T(8,128)(2,1)S(1)}, bf16[8,264,128]{2,1,0:T(8,128)(2,1)}, u32[]{:S(2)}) copy-start(bf16[8,264,128]{2,1,0:T(8,128)(2,1)} %copy-done.5) | copy-start | bytes 1622020
  65.0 25.9 %copy-start = (bf16[16,264,128]{2,1,0:T(8,128)(2,1)}, bf16[16,264,128]{2,1,0:T(8,128)(2,1)S(1)}, u32[]{:S(2)}) copy-start(bf16[16,264,128]{2,1,0:T(8,128)(2,1)S(1)} %all-to-all-done.1.recv.refs_5_) | copy-start | bytes 3244036
  65.0 30.4 %all-to-all-start.2 = ((bf16[16,264,128]{2,1,0:T(8,128)(2,1)}), bf16[16,264,128]{2,1,0:T(8,128)(2,1)S(1)}, u32[]{:S(2)}, u32[]{:S(2)}) async-start(bf16[16,264,128]{2,1,0:T(8,128)(2,1)} %pick.6), calls=%async_computation.2 | async-start | bytes 2162688 | tf_op jit(solution)/shard_map/all_to_all | solution.py:397
  70.0 16.9 %collective-permute-start.6 = (bf16[8,264,128]{2,1,0:T(8,128)(2,1)S(1)}, bf16[8,264,128]{2,1,0:T(8,128)(2,1)}, u32[]{:S(2)}, u32[]{:S(2)}) collective-permute-start(bf16[8,264,128]{2,1,0:T(8,128)(2,1)S(1)} %copy-done.6), channel_id=1, source_target_pairs={{0,7},{1,0},{2,1},{3,2},{4,3},{5,4},{6,5},{7,6},{8,15},{9,8},{10,9... | collective-permute-start | bytes 1622024 | tf_op jit(solution)/shard_map/ppermute | solution.py:359
  75.1 11.8 %copy-start.7 = (bf16[8,264,128]{2,1,0:T(8,128)(2,1)}, bf16[8,264,128]{2,1,0:T(8,128)(2,1)S(1)}, u32[]{:S(2)}) copy-start(bf16[8,264,128]{2,1,0:T(8,128)(2,1)S(1)} %collective-permute-done.4.refs_0_) | copy-start | bytes 1622020
  75.1 17.2 %collective-permute-start.5 = (bf16[8,264,128]{2,1,0:T(8,128)(2,1)S(1)}, bf16[8,264,128]{2,1,0:T(8,128)(2,1)}, u32[]{:S(2)}, u32[]{:S(2)}) collective-permute-start(bf16[8,264,128]{2,1,0:T(8,128)(2,1)S(1)} %collective-permute-done.4.refs_0_), channel_id=1, source_target_pairs={{0,1},{1,2},{2,3},{3,4},{4,5},{5,6},{6,7},{7,0},{8,9},{9,10},{10,1... | collective-permute-start | bytes 1622024 | tf_op jit(solution)/shard_map/ppermute | solution.py:359
  95.4 1.1 copy-start.1
  96.5 26.2 %all-to-all-start.3 = ((bf16[24,264,128]{2,1,0:T(8,128)(2,1)}), bf16[24,264,128]{2,1,0:T(8,128)(2,1)}, u32[]{:S(2)}, u32[]{:S(2)}) async-start(bf16[24,264,128]{2,1,0:T(8,128)(2,1)} %add.1), calls=%async_computation.3 | async-start | bytes 3244032 | tf_op jit(solution)/shard_map/all_to_all | solution.py:397
